TPU v7x, 32 devices: a whole 2x2x4 slice. The times are simulated.
32 devices in a mesh: ia: 4 (over y, x), ja: 2 (over core), ka: 4 (over z).
Axes of the slice: x: 2, y: 2, z: 4, core: 2. Of those that a mesh axis runs over, the one named last changes fastest.
Arguments:
- tensor: bfloat16 [128, 256, 1024], P('ia', 'ja', 'ka'), may hold values from 5 to 200
- factor_first: bfloat16 [128, 256], P('ia', ('ja', 'ka')), may hold values from 0.19921875 to 1.5
- factor_second: bfloat16 [256, 256], P('ja', ('ia', 'ka')), may hold values from 0.19921875 to 1.5
- factor_third: bfloat16 [1024, 256], P('ka', ('ia', 'ja')), may hold values from 0.19921875 to 1.5
Outputs:
- grad_first: float32 [128, 256], P('ia', ('ja', 'ka'))
- grad_second: float32 [256, 256], P('ja', ('ia', 'ka'))
- grad_third: float32 [1024, 256], P('ka', ('ia', 'ja'))
All inputs are finite; a program needn't handle non-finite values.
Results may differ from a plain program's by a relative error of at most 0.005.
Values may be sent and summed in bfloat16 or wider, within the bound.
No kernel may reach another device: no remote copies, remote signals or barrier semaphores. Data moves between devices by JAX's collectives and lax.ppermute only.
A program may use at most 64 MiB of HBM per device.

v0:
```python
import jax
import jax.numpy as jnp
from jax import lax
from jax.sharding import PartitionSpec as P


def body(tensor, factor_first, factor_second, factor_third):
    full_first = lax.all_gather(factor_first, ("ja", "ka"), axis=1, tiled=True)
    full_second = lax.all_gather(factor_second, ("ia", "ka"), axis=1, tiled=True)
    full_third = lax.all_gather(factor_third, ("ia", "ja"), axis=1, tiled=True)
    rows_i, rows_j, rows_k = tensor.shape
    rank = full_first.shape[1]
    total_i = rows_i * lax.axis_size("ia")
    total_j = rows_j * lax.axis_size("ja")
    total_k = rows_k * lax.axis_size("ka")
    first32 = full_first.astype(jnp.float32)
    second32 = full_second.astype(jnp.float32)
    khatri = (first32[:, None, :] * second32[None, :, :]).astype(jnp.bfloat16)
    khatri_flat = khatri.reshape(rows_i * rows_j, rank)
    model = jnp.einsum("mr,kr->mk", khatri_flat, full_third, preferred_element_type=jnp.float32)
    flat_data = tensor.reshape(rows_i * rows_j, rows_k).astype(jnp.float32)
    deriv = ((model - flat_data) * lax.rsqrt(model)).astype(jnp.bfloat16)
    part_third = jnp.einsum("mk,mr->kr", deriv, khatri_flat, preferred_element_type=jnp.float32)
    inner = jnp.einsum("mk,kr->mr", deriv, full_third, preferred_element_type=jnp.float32)
    inner = inner.reshape(rows_i, rows_j, rank)
    part_first = jnp.sum(inner * second32[None, :, :], axis=1) / (total_j * total_k)
    part_second = jnp.sum(inner * first32[:, None, :], axis=0) / (total_i * total_k)
    part_third = part_third / (total_i * total_j)
    grad_first = lax.psum_scatter(part_first, ("ja", "ka"), scatter_dimension=1, tiled=True)
    grad_second = lax.psum_scatter(part_second, ("ia", "ka"), scatter_dimension=1, tiled=True)
    grad_third = lax.psum_scatter(part_third, ("ia", "ja"), scatter_dimension=1, tiled=True)
    return (grad_first, grad_second, grad_third)


def solution(mesh):
    placed = (
        P("ia", "ja", "ka"),
        P("ia", ("ja", "ka")),
        P("ja", ("ia", "ka")),
        P("ka", ("ia", "ja")),
    )
    return jax.shard_map(
        body,
        mesh=mesh,
        in_specs=placed,
        out_specs=(P("ia", ("ja", "ka")), P("ja", ("ia", "ka")), P("ka", ("ia", "ja"))),
        check_vma=False,
    )
```

profile of v0, /device:TPU:0, one launch (start us, length us, event | category | flops | bytes accessed | tf_op | source)
XLA Modules:
  0.0 234.9 jit_solution(1074803909325882737)
XLA Ops:
  7.2 0.0 reduce-scatter.10.cloned.1.call-start
  7.2 0.8 copy.16
  8.0 25.6 %all_gather.9 = bf16[32,256]{0,1:T(8,128)(2,1)S(1)} all-gather(bf16[32,32]{0,1:T(8,128)(2,1)S(1)} %copy.16), channel_id=1, replica_groups=mesh['ia'=4,'ja'=2,'ka'=4] {'ja','ka'}, dimensions={1}, use_global_device_ids=true | all-gather | bytes 18432 | tf_op jit(solution)/shard_map/all_gather | solution.py:8
  33.6 0.1 copy.17
  33.7 41.3 %all_gather.10 = bf16[128,256]{0,1:T(8,128)(2,1)S(1)} all-gather(bf16[128,16]{0,1:T(8,128)(2,1)} %param.6), channel_id=1, replica_groups=mesh['ia'=4,'ja'=2,'ka'=4] {'ia','ka'}, dimensions={1}, use_global_device_ids=true | all-gather | bytes 69632 | tf_op jit(solution)/shard_map/all_gather | solution.py:9
  75.0 0.1 copy.18
  75.1 8.5 %all_gather.11 = bf16[256,256]{0,1:T(8,128)(2,1)S(1)} all-gather(bf16[256,32]{0,1:T(8,128)(2,1)} %param.7), channel_id=1, replica_groups=mesh['ia'=4,'ja'=2,'ka'=4] {'ia','ja'}, dimensions={1}, use_global_device_ids=true | all-gather | bytes 147456 | tf_op jit(solution)/shard_map/all_gather | solution.py:10
  83.6 0.6 multiply_convert_fusion
  84.3 0.9 fusion.1
  85.2 0.4 copy-done
  85.6 2.7 %multiply_reduce_fusion.1 = (f32[32,256]{1,0:T(8,128)S(1)}, f32[4096,256]{1,0:T(8,128)}) fusion(f32[128,256]{1,0:T(8,128)S(1)} %copy.18, bf16[4096,256]{1,0:T(8,128)(2,1)S(1)} %fusion.1, bf16[256,256]{0,1:T(8,128)(2,1)S(1)} %all_gather.11), kind=kOutput, calls=%fused_computation.4 | convolution fusion | flops 538959872 | bytes 6586368 | tf_op jit(solution)/shard_map/mk,kr->mr/dot_general | solution.py:24
  88.3 0.7 copy.20
  89.0 0.0 reduce-scatter.10.cloned.1.call-update
  89.0 0.0 reduce-scatter.12.cloned.1.call-start
  89.1 2.6 %multiply_reduce_fusion = f32[128,256]{1,0:T(8,128)S(1)} fusion(f32[32,128,256]{2,1,0:T(8,128)} %bitcast.16, f32[32,256]{1,0:T(8,128)S(1)} %convert_element_type.22), kind=kLoop, calls=%fused_computation.3 | loop fusion | flops 2064384 | bytes 4358144 | tf_op jit(solution)/shard_map/reduce_sum | solution.py:27
  91.7 0.8 copy.22
  92.4 0.0 reduce-scatter.12.cloned.1.call-update
  92.5 0.0 reduce-scatter.8.cloned.1.call-start
  92.5 3.2 %convolution_multiply_fusion = f32[256,256]{0,1:T(8,128)} fusion(bf16[4096,256]{1,0:T(8,128)(2,1)S(1)} %fusion.1, bf16[4096,256]{1,0:T(8,128)(2,1)} %bitcast.18), kind=kOutput, calls=%fused_computation.6 | convolution fusion | flops 536936448 | bytes 4456448 | tf_op jit(solution)/shard_map/mk,mr->kr/dot_general | solution.py:23
  95.7 0.0 reduce-scatter.8.cloned.1.call-update
  95.7 21.5 %reduce-scatter.10.cloned.1.call-done = f32[32,32]{1,0:T(8,128)} async-done(((f32[256,32]{1,0:T(8,128)}), f32[32,32]{1,0:T(8,128)}) %reduce-scatter.10.cloned.1.call-update) | async-done | bytes 4112
  117.3 1.4 copy.21
  118.7 75.9 %reduce-scatter.12.cloned.1.call-done = f32[16,128]{1,0:T(8,128)} async-done(((f32[256,128]{1,0:T(8,128)}), f32[16,128]{1,0:T(8,128)}) %reduce-scatter.12.cloned.1.call-update) | async-done | bytes 8208
  194.6 33.8 %reduce-scatter.8.cloned.1.call-done = f32[256,32]{0,1:T(8,128)} async-done(((f32[256,256]{0,1:T(8,128)}), f32[256,32]{0,1:T(8,128)}) %reduce-scatter.8.cloned.1.call-update) | async-done | bytes 32784 | tf_op jit(solution)/shard_map/reduce_scatter | solution.py:31
  (6 shorter events, 0.0 us)
Async XLA Ops:
  7.2 110.1 %reduce-scatter.10.cloned.1.call-start = ((), (), s32[]{:S(2)}) async-start(), calls=%async_computation.4 | async-start | bytes 147456
  75.1 9.2 %copy-start.1 = (bf16[32,128,256]{2,1,0:T(8,128)(2,1)S(1)}, bf16[32,128,256]{2,1,0:T(8,128)(2,1)}, u32[]{:S(2)}) copy-start(bf16[32,128,256]{2,1,0:T(8,128)(2,1)} %param.4) | copy-start | bytes 6291460
  84.3 1.3 copy-start
  89.0 105.6 %reduce-scatter.12.cloned.1.call-start = ((), (), s32[]{:S(2)}) async-start(), calls=%async_computation.5 | async-start | bytes 139264
  92.5 136.0 %reduce-scatter.8.cloned.1.call-start = ((), (), s32[]{:S(2)}) async-start(), calls=%async_computation.3 | async-start | bytes 294912 | tf_op jit(solution)/shard_map/reduce_scatter | solution.py:31
Sparse Core Ops, SparseCore 0:
  89.2 28.0 reduce-scatter.9
  120.2 74.3 reduce-scatter.11
  198.2 30.1 reduce-scatter.7
where the time goes:
time: 235 us
  waiting for transfers between devices  131 us (56%)
  blocking collectives  75.4 us (32%)
  between operations  13.8 us (6%)
  matrix products  6.78 us (3%)
  local copies, waits for them, and re-layouts  4.27 us (2%)
  other arithmetic  3.22 us (1%)
    unnamed x5, waiting for transfers between devices  97.5 us
    all_gather x1, blocking collectives, body(): lax.all_gather(factor_second, ('ia', 'ka'), axis=1, tiled=True)  41.3 us
    reduce_scatter x1, waiting for transfers between devices, body(): lax.psum_scatter(part_third, ('ia', 'ja'), scatter_dimension=1, tiled=True)  33.8 us
    all_gather x1, blocking collectives, body(): full_first = lax.all_gather(factor_first, ('ja', 'ka'), axis=1, tiled=True)  25.6 us
    all_gather x1, blocking collectives, body(): full_third = lax.all_gather(factor_third, ('ia', 'ja'), axis=1, tiled=True)  8.54 us
  transfers between devices with their start and end apart: 3, of which 3 were waited for; matrix products, arithmetic and copies ran while one was open for 3% of the time, Pallas kernels for 0%

commit v1 on v0

--- a/solution.py
+++ b/solution.py
@@ -4,9 +4,30 @@
 from jax.sharding import PartitionSpec as P
 
 
+def gather_around(value, axis, dim):
+    peers, index, span = (lax.axis_size(axis), lax.axis_index(axis), value.shape[dim])
+    ahead = [(i, (i + 1) % peers) for i in range(peers)]
+    downward = [(i, (i - 1) % peers) for i in range(peers)]
+    result = jnp.zeros((*value.shape[:dim], peers * span, *value.shape[dim + 1 :]), value.dtype)
+    result = lax.dynamic_update_slice_in_dim(result, value, index * span, axis=dim)
+    from_left = from_right = value
+    halfway = peers // 2
+    for step in range(1, halfway + 1):
+        from_left = lax.ppermute(from_left, axis, ahead)
+        result = lax.dynamic_update_slice_in_dim(
+            result, from_left, (index - step) % peers * span, axis=dim
+        )
+        if step < peers - halfway:
+            from_right = lax.ppermute(from_right, axis, downward)
+            result = lax.dynamic_update_slice_in_dim(
+                result, from_right, (index + step) % peers * span, axis=dim
+            )
+    return result
+
+
 def body(tensor, factor_first, factor_second, factor_third):
     full_first = lax.all_gather(factor_first, ("ja", "ka"), axis=1, tiled=True)
-    full_second = lax.all_gather(factor_second, ("ia", "ka"), axis=1, tiled=True)
+    full_second = gather_around(factor_second, ("ia", "ka"), 1)
     full_third = lax.all_gather(factor_third, ("ia", "ja"), axis=1, tiled=True)
     rows_i, rows_j, rows_k = tensor.shape
     rank = full_first.shape[1]

time: 235 us -> 255 us (1.085)
  blocking collectives: 75.4 us -> 33.1 us
  starting transfers between devices: 0.12 us -> 41.5 us
  waiting for transfers between devices: 131 us -> 145 us
  local copies, waits for them, and re-layouts: 4.27 us -> 13.9 us
    ppermute x0 -> x15, starting transfers between devices: none -> 41.4 us  [the longest x7 38.3 us: gather_around(): from_right = lax.ppermute(from_right, axis, downward)]
    all_gather x1 -> x0, blocking collectives: 41.3 us -> none  [body(): lax.all_gather(factor_second, ('ia', 'ka'), axis=1, tiled=True)]
    ppermute x0 -> x15, waiting for transfers between devices: none -> 6.78 us  [the longest x8 4.9 us: gather_around(): from_left = lax.ppermute(from_left, axis, ahead)]
    unnamed x5, waiting for transfers between devices: 97.5 us -> 104 us
    dynamic_update_slice x0 -> x16, local copies, waits for them, and re-layouts: none -> 6.22 us  [the longest x7 3 us: gather_around(): lax.dynamic_update_slice_in_dim(result, from_right, (index + step) % peer...]
    unnamed x8 -> x7, local copies, waits for them, and re-layouts: 4.1 us -> 5.78 us
  transfers between devices with their start and end apart: 3 -> 18, of which waited for: 3 -> 8; matrix products, arithmetic and copies ran while one was open for 3% -> 6% of each run, Pallas kernels for 0% -> 0%
where the time goes in v1:
time: 255 us
  waiting for transfers between devices  145 us (57%)
  starting transfers between devices  41.5 us (16%)
  blocking collectives  33.1 us (13%)
  between operations  14.1 us (6%)
  local copies, waits for them, and re-layouts  13.9 us (5%)
  matrix products  6.4 us (3%)
    unnamed x5, waiting for transfers between devices  104 us
    ppermute x7, starting transfers between devices, gather_around(): from_right = lax.ppermute(from_right, axis, downward)  38.3 us
    reduce_scatter x1, waiting for transfers between devices, body(): lax.psum_scatter(part_third, ('ia', 'ja'), scatter_dimension=1, tiled=True)  33.6 us
    all_gather x1, blocking collectives, body(): full_first = lax.all_gather(factor_first, ('ja', 'ka'), axis=1, tiled=True)  23.8 us
    all_gather x1, blocking collectives, body(): full_third = lax.all_gather(factor_third, ('ia', 'ja'), axis=1, tiled=True)  9.31 us
    unnamed x7, local copies, waits for them, and re-layouts  5.78 us
  transfers between devices with their start and end apart: 18, of which 8 were waited for; matrix products, arithmetic and copies ran while one was open for 6% of the time, Pallas kernels for 0%

profile of v1, /device:TPU:0, one launch (start us, length us, event | category | flops | bytes accessed | tf_op | source)
XLA Modules:
  0.0 254.8 jit_solution(17053710485362711936)
XLA Ops:
  7.2 3.1 %collective-permute-start = (bf16[128,16]{0,1:T(8,128)(2,1)}, bf16[128,16]{0,1:T(8,128)(2,1)S(1)}, u32[]{:S(2)}, u32[]{:S(2)}) collective-permute-start(bf16[128,16]{0,1:T(8,128)(2,1)} %param.6), channel_id=1, source_target_pairs={{0,1},{1,2},{2,3},{3,8},{8,9},{9,10},{10,11},{11,16},{16,17},{17,1... | collective-permute-start | bytes 12296 | tf_op jit(solution)/shard_map/ppermute | solution.py:16
  10.3 4.0 %collective-permute-start.1 = (bf16[128,16]{0,1:T(8,128)(2,1)}, bf16[128,16]{0,1:T(8,128)(2,1)S(1)}, u32[]{:S(2)}, u32[]{:S(2)}) collective-permute-start(bf16[128,16]{0,1:T(8,128)(2,1)} %param.6), channel_id=1, source_target_pairs={{0,27},{1,0},{2,1},{3,2},{8,3},{9,8},{10,9},{11,10},{16,11},{17,16... | collective-permute-start | bytes 12296 | tf_op jit(solution)/shard_map/ppermute | solution.py:21
  14.3 1.8 collective-permute-done
  16.0 5.6 %collective-permute-start.3 = (bf16[128,16]{0,1:T(8,128)(2,1)S(1)}, bf16[128,16]{0,1:T(8,128)(2,1)S(1)}, u32[]{:S(2)}, u32[]{:S(2)}) collective-permute-start(bf16[128,16]{0,1:T(8,128)(2,1)S(1)} %collective-permute-done.1), channel_id=1, source_target_pairs={{0,27},{1,0},{2,1},{3,2},{8,3},{9,8},{10,9},{11,10},{16,11},{17,16... | collective-permute-start | bytes 12296 | tf_op jit(solution)/shard_map/ppermute | solution.py:21
  21.7 1.6 collective-permute-done.2
  23.2 5.6 %collective-permute-start.5 = (bf16[128,16]{0,1:T(8,128)(2,1)S(1)}, bf16[128,16]{0,1:T(8,128)(2,1)S(1)}, u32[]{:S(2)}, u32[]{:S(2)}) collective-permute-start(bf16[128,16]{0,1:T(8,128)(2,1)S(1)} %collective-permute-done.3), channel_id=1, source_target_pairs={{0,27},{1,0},{2,1},{3,2},{8,3},{9,8},{10,9},{11,10},{16,11},{17,16... | collective-permute-start | bytes 12296 | tf_op jit(solution)/shard_map/ppermute | solution.py:21
  28.9 1.6 collective-permute-done.4
  30.4 9.3 %all_gather.7 = bf16[256,256]{0,1:T(8,128)(2,1)S(1)} all-gather(bf16[256,32]{0,1:T(8,128)(2,1)} %param.7), channel_id=1, replica_groups=mesh['ia'=4,'ja'=2,'ka'=4] {'ia','ja'}, dimensions={1}, use_global_device_ids=true | all-gather | bytes 147456 | tf_op jit(solution)/shard_map/all_gather | solution.py:31
  39.7 5.6 %collective-permute-start.7 = (bf16[128,16]{0,1:T(8,128)(2,1)S(1)}, bf16[128,16]{0,1:T(8,128)(2,1)S(1)}, u32[]{:S(2)}, u32[]{:S(2)}) collective-permute-start(bf16[128,16]{0,1:T(8,128)(2,1)S(1)} %collective-permute-done.5), channel_id=1, source_target_pairs={{0,27},{1,0},{2,1},{3,2},{8,3},{9,8},{10,9},{11,10},{16,11},{17,16... | collective-permute-start | bytes 12296 | tf_op jit(solution)/shard_map/ppermute | solution.py:21
  45.4 1.3 collective-permute-done.7
  46.7 5.9 %collective-permute-start.9 = (bf16[128,16]{0,1:T(8,128)(2,1)S(1)}, bf16[128,16]{0,1:T(8,128)(2,1)S(1)}, u32[]{:S(2)}, u32[]{:S(2)}) collective-permute-start(bf16[128,16]{0,1:T(8,128)(2,1)S(1)} %collective-permute-done.7), channel_id=1, source_target_pairs={{0,27},{1,0},{2,1},{3,2},{8,3},{9,8},{10,9},{11,10},{16,11},{17,16... | collective-permute-start | bytes 12296 | tf_op jit(solution)/shard_map/ppermute | solution.py:21
  52.6 0.8 copy.61
  53.9 5.9 %collective-permute-start.11 = (bf16[128,16]{0,1:T(8,128)(2,1)S(1)}, bf16[128,16]{0,1:T(8,128)(2,1)S(1)}, u32[]{:S(2)}, u32[]{:S(2)}) collective-permute-start(bf16[128,16]{0,1:T(8,128)(2,1)S(1)} %collective-permute-done.9), channel_id=1, source_target_pairs={{0,27},{1,0},{2,1},{3,2},{8,3},{9,8},{10,9},{11,10},{16,11},{17,16... | collective-permute-start | bytes 12296 | tf_op jit(solution)/shard_map/ppermute | solution.py:21
  59.8 23.8 %all_gather.6 = bf16[32,256]{0,1:T(8,128)(2,1)S(1)} all-gather(bf16[32,32]{0,1:T(8,128)(2,1)S(1)} %copy.61), channel_id=1, replica_groups=mesh['ia'=4,'ja'=2,'ka'=4] {'ja','ka'}, dimensions={1}, use_global_device_ids=true | all-gather | bytes 18432 | tf_op jit(solution)/shard_map/all_gather | solution.py:29
  83.6 5.7 %collective-permute-start.13 = (bf16[128,16]{0,1:T(8,128)(2,1)S(1)}, bf16[128,16]{0,1:T(8,128)(2,1)S(1)}, u32[]{:S(2)}, u32[]{:S(2)}) collective-permute-start(bf16[128,16]{0,1:T(8,128)(2,1)S(1)} %collective-permute-done.11), channel_id=1, source_target_pairs={{0,27},{1,0},{2,1},{3,2},{8,3},{9,8},{10,9},{11,10},{16,11},{17,16... | collective-permute-start | bytes 12296 | tf_op jit(solution)/shard_map/ppermute | solution.py:21
  89.3 0.8 copy.63
  99.2 1.3 copy-done
  100.5 2.4 fusion.1
  102.9 0.8 multiply_reduce_fusion.1
  105.8 3.2 %convolution_multiply_fusion = f32[256,256]{0,1:T(8,128)} fusion(bf16[4096,256]{1,0:T(8,128)(2,1)S(1)} %fusion.1, bf16[4096,256]{1,0:T(8,128)(2,1)} %bitcast.18), kind=kOutput, calls=%fused_computation.6 | convolution fusion | flops 536936448 | bytes 4456448 | tf_op jit(solution)/shard_map/mk,mr->kr/dot_general | solution.py:44
  109.1 28.2 %reduce-scatter.10.cloned.1.call-done = f32[32,32]{1,0:T(8,128)} async-done(((f32[256,32]{1,0:T(8,128)}), f32[32,32]{1,0:T(8,128)}) %reduce-scatter.10.cloned.1.call-update) | async-done | bytes 4112
  137.3 1.4 copy.81
  138.6 76.0 %reduce-scatter.12.cloned.1.call-done = f32[16,128]{1,0:T(8,128)} async-done(((f32[256,128]{1,0:T(8,128)}), f32[16,128]{1,0:T(8,128)}) %reduce-scatter.12.cloned.1.call-update) | async-done | bytes 8208
  214.6 33.6 %reduce-scatter.8.cloned.1.call-done = f32[256,32]{0,1:T(8,128)} async-done(((f32[256,256]{0,1:T(8,128)}), f32[256,32]{0,1:T(8,128)}) %reduce-scatter.8.cloned.1.call-update) | async-done | bytes 32784 | tf_op jit(solution)/shard_map/reduce_scatter | solution.py:52
  (66 shorter events, 11.6 us)
Async XLA Ops:
  7.2 130.1 %reduce-scatter.10.cloned.1.call-start = ((), (), s32[]{:S(2)}) async-start(), calls=%async_computation.4 | async-start | bytes 147456
  7.2 8.8 %collective-permute-start = (bf16[128,16]{0,1:T(8,128)(2,1)}, bf16[128,16]{0,1:T(8,128)(2,1)S(1)}, u32[]{:S(2)}, u32[]{:S(2)}) collective-permute-start(bf16[128,16]{0,1:T(8,128)(2,1)} %param.6), channel_id=1, source_target_pairs={{0,1},{1,2},{2,3},{3,8},{8,9},{9,10},{10,11},{11,16},{16,17},{17,1... | collective-permute-start | bytes 12296 | tf_op jit(solution)/shard_map/ppermute | solution.py:16
  10.3 5.8 %collective-permute-start.1 = (bf16[128,16]{0,1:T(8,128)(2,1)}, bf16[128,16]{0,1:T(8,128)(2,1)S(1)}, u32[]{:S(2)}, u32[]{:S(2)}) collective-permute-start(bf16[128,16]{0,1:T(8,128)(2,1)} %param.6), channel_id=1, source_target_pairs={{0,27},{1,0},{2,1},{3,2},{8,3},{9,8},{10,9},{11,10},{16,11},{17,16... | collective-permute-start | bytes 12296 | tf_op jit(solution)/shard_map/ppermute | solution.py:21
  16.0 7.2 %collective-permute-start.2 = (bf16[128,16]{0,1:T(8,128)(2,1)S(1)}, bf16[128,16]{0,1:T(8,128)(2,1)S(1)}, u32[]{:S(2)}, u32[]{:S(2)}) collective-permute-start(bf16[128,16]{0,1:T(8,128)(2,1)S(1)} %collective-permute-done), channel_id=1, source_target_pairs={{0,1},{1,2},{2,3},{3,8},{8,9},{9,10},{10,11},{11,16},{16,17},{17,1... | collective-permute-start | bytes 12296 | tf_op jit(solution)/shard_map/ppermute | solution.py:16
  16.0 7.2 %collective-permute-start.3 = (bf16[128,16]{0,1:T(8,128)(2,1)S(1)}, bf16[128,16]{0,1:T(8,128)(2,1)S(1)}, u32[]{:S(2)}, u32[]{:S(2)}) collective-permute-start(bf16[128,16]{0,1:T(8,128)(2,1)S(1)} %collective-permute-done.1), channel_id=1, source_target_pairs={{0,27},{1,0},{2,1},{3,2},{8,3},{9,8},{10,9},{11,10},{16,11},{17,16... | collective-permute-start | bytes 12296 | tf_op jit(solution)/shard_map/ppermute | solution.py:21
  23.2 7.2 %collective-permute-start.4 = (bf16[128,16]{0,1:T(8,128)(2,1)S(1)}, bf16[128,16]{0,1:T(8,128)(2,1)S(1)}, u32[]{:S(2)}, u32[]{:S(2)}) collective-permute-start(bf16[128,16]{0,1:T(8,128)(2,1)S(1)} %collective-permute-done.2), channel_id=1, source_target_pairs={{0,1},{1,2},{2,3},{3,8},{8,9},{9,10},{10,11},{11,16},{16,17},{17,1... | collective-permute-start | bytes 12296 | tf_op jit(solution)/shard_map/ppermute | solution.py:16
  23.2 16.5 %collective-permute-start.5 = (bf16[128,16]{0,1:T(8,128)(2,1)S(1)}, bf16[128,16]{0,1:T(8,128)(2,1)S(1)}, u32[]{:S(2)}, u32[]{:S(2)}) collective-permute-start(bf16[128,16]{0,1:T(8,128)(2,1)S(1)} %collective-permute-done.3), channel_id=1, source_target_pairs={{0,27},{1,0},{2,1},{3,2},{8,3},{9,8},{10,9},{11,10},{16,11},{17,16... | collective-permute-start | bytes 12296 | tf_op jit(solution)/shard_map/ppermute | solution.py:21
  30.4 15.0 %collective-permute-start.6 = (bf16[128,16]{0,1:T(8,128)(2,1)S(1)}, bf16[128,16]{0,1:T(8,128)(2,1)S(1)}, u32[]{:S(2)}, u32[]{:S(2)}) collective-permute-start(bf16[128,16]{0,1:T(8,128)(2,1)S(1)} %collective-permute-done.4), channel_id=1, source_target_pairs={{0,1},{1,2},{2,3},{3,8},{8,9},{9,10},{10,11},{11,16},{16,17},{17,1... | collective-permute-start | bytes 12296 | tf_op jit(solution)/shard_map/ppermute | solution.py:16
  39.7 7.0 %collective-permute-start.7 = (bf16[128,16]{0,1:T(8,128)(2,1)S(1)}, bf16[128,16]{0,1:T(8,128)(2,1)S(1)}, u32[]{:S(2)}, u32[]{:S(2)}) collective-permute-start(bf16[128,16]{0,1:T(8,128)(2,1)S(1)} %collective-permute-done.5), channel_id=1, source_target_pairs={{0,27},{1,0},{2,1},{3,2},{8,3},{9,8},{10,9},{11,10},{16,11},{17,16... | collective-permute-start | bytes 12296 | tf_op jit(solution)/shard_map/ppermute | solution.py:21
  45.4 7.2 %collective-permute-start.8 = (bf16[128,16]{0,1:T(8,128)(2,1)S(1)}, bf16[128,16]{0,1:T(8,128)(2,1)S(1)}, u32[]{:S(2)}, u32[]{:S(2)}) collective-permute-start(bf16[128,16]{0,1:T(8,128)(2,1)S(1)} %collective-permute-done.6), channel_id=1, source_target_pairs={{0,1},{1,2},{2,3},{3,8},{8,9},{9,10},{10,11},{11,16},{16,17},{17,1... | collective-permute-start | bytes 12296 | tf_op jit(solution)/shard_map/ppermute | solution.py:16
  46.7 7.2 %collective-permute-start.9 = (bf16[128,16]{0,1:T(8,128)(2,1)S(1)}, bf16[128,16]{0,1:T(8,128)(2,1)S(1)}, u32[]{:S(2)}, u32[]{:S(2)}) collective-permute-start(bf16[128,16]{0,1:T(8,128)(2,1)S(1)} %collective-permute-done.7), channel_id=1, source_target_pairs={{0,27},{1,0},{2,1},{3,2},{8,3},{9,8},{10,9},{11,10},{16,11},{17,16... | collective-permute-start | bytes 12296 | tf_op jit(solution)/shard_map/ppermute | solution.py:21
  52.6 7.2 %collective-permute-start.10 = (bf16[128,16]{0,1:T(8,128)(2,1)S(1)}, bf16[128,16]{0,1:T(8,128)(2,1)S(1)}, u32[]{:S(2)}, u32[]{:S(2)}) collective-permute-start(bf16[128,16]{0,1:T(8,128)(2,1)S(1)} %collective-permute-done.8), channel_id=1, source_target_pairs={{0,1},{1,2},{2,3},{3,8},{8,9},{9,10},{10,11},{11,16},{16,17},{17,1... | collective-permute-start | bytes 12296 | tf_op jit(solution)/shard_map/ppermute | solution.py:16
  53.9 29.7 %collective-permute-start.11 = (bf16[128,16]{0,1:T(8,128)(2,1)S(1)}, bf16[128,16]{0,1:T(8,128)(2,1)S(1)}, u32[]{:S(2)}, u32[]{:S(2)}) collective-permute-start(bf16[128,16]{0,1:T(8,128)(2,1)S(1)} %collective-permute-done.9), channel_id=1, source_target_pairs={{0,27},{1,0},{2,1},{3,2},{8,3},{9,8},{10,9},{11,10},{16,11},{17,16... | collective-permute-start | bytes 12296 | tf_op jit(solution)/shard_map/ppermute | solution.py:21
  59.8 29.5 %collective-permute-start.12 = (bf16[128,16]{0,1:T(8,128)(2,1)S(1)}, bf16[128,16]{0,1:T(8,128)(2,1)S(1)}, u32[]{:S(2)}, u32[]{:S(2)}) collective-permute-start(bf16[128,16]{0,1:T(8,128)(2,1)S(1)} %collective-permute-done.10), channel_id=1, source_target_pairs={{0,1},{1,2},{2,3},{3,8},{8,9},{9,10},{10,11},{11,16},{16,17},{17,1... | collective-permute-start | bytes 12296 | tf_op jit(solution)/shard_map/ppermute | solution.py:16
  83.6 14.0 %collective-permute-start.13 = (bf16[128,16]{0,1:T(8,128)(2,1)S(1)}, bf16[128,16]{0,1:T(8,128)(2,1)S(1)}, u32[]{:S(2)}, u32[]{:S(2)}) collective-permute-start(bf16[128,16]{0,1:T(8,128)(2,1)S(1)} %collective-permute-done.11), channel_id=1, source_target_pairs={{0,27},{1,0},{2,1},{3,2},{8,3},{9,8},{10,9},{11,10},{16,11},{17,16... | collective-permute-start | bytes 12296 | tf_op jit(solution)/shard_map/ppermute | solution.py:21
  89.3 8.9 %collective-permute-start.14 = (bf16[128,16]{0,1:T(8,128)(2,1)S(1)}, bf16[128,16]{0,1:T(8,128)(2,1)S(1)}, u32[]{:S(2)}, u32[]{:S(2)}) collective-permute-start(bf16[128,16]{0,1:T(8,128)(2,1)S(1)} %collective-permute-done.12), channel_id=1, source_target_pairs={{0,1},{1,2},{2,3},{3,8},{8,9},{9,10},{10,11},{11,16},{16,17},{17,1... | collective-permute-start | bytes 12296 | tf_op jit(solution)/shard_map/ppermute | solution.py:16
  99.1 1.3 copy-start
  104.9 109.7 %reduce-scatter.12.cloned.1.call-start = ((), (), s32[]{:S(2)}) async-start(), calls=%async_computation.5 | async-start | bytes 139264
  105.8 142.5 %reduce-scatter.8.cloned.1.call-start = ((), (), s32[]{:S(2)}) async-start(), calls=%async_computation.3 | async-start | bytes 294912 | tf_op jit(solution)/shard_map/reduce_scatter | solution.py:52
Sparse Core Ops, SparseCore 0:
  105.1 32.1 reduce-scatter.9
  140.1 74.4 reduce-scatter.11
  218.2 29.9 reduce-scatter.7
